TPU v7x, 256 devices: a whole 4x4x8 slice. The times are simulated.
256 devices in a mesh: row: 8 (over y, z_lo), col: 32 (over z_hi, x, core).
Axes of the slice: x: 4, y: 4, z: 8 (z_hi: 4, z_lo: 2; z = z_hi * 2 + z_lo), core: 2. Of those that a mesh axis runs over, the one named last changes fastest.
Arguments:
- grad_output: bfloat16 [1024, 8192], P('col', 'row'), may hold values from -6 to 6
- inputs: bfloat16 [1024, 28672], P('row', 'col'), may hold values from -0.1875 to 0.1875
- weight: bfloat16 [28672, 8192], P('col', 'row'), may hold values from -0.125 to 0.125
- block_mask: int32 [224, 64], P('col'), may hold values from 0 to 1, as said below
Outputs:
- grad_input: bfloat16 [1024, 28672], P('row', 'col')
- grad_weight: bfloat16 [28672, 8192], P('col', 'row')
Inputs may be any that keep to these rules, and one draw needn't show every extreme that they name: `block_mask`: 1 where the 128 x 128 block of weight is kept, 0 where it is zero; the share of kept blocks differs widely from block row to block row.
All inputs are finite; a program needn't handle non-finite values.
Results may differ from a plain program's by a relative error of at most 0.001.
Values may be sent and summed in bfloat16 or wider, within the bound.
A program may use at most 64 MiB of HBM per device.

v0:
```python
import jax
import jax.numpy as jnp
from jax import lax
from jax.sharding import PartitionSpec as P

BLOCK = 128


def joined_along(parts, dim):
    parts = jnp.moveaxis(parts, 0, dim)
    shape = parts.shape
    return parts.reshape(*shape[:dim], shape[dim] * shape[dim + 1], *shape[dim + 2 :])


def sent_to_all(x, axis):
    size = lax.axis_size(axis)
    return lax.all_to_all(jnp.broadcast_to(x[None], (size, *x.shape)), axis, 0, 0, tiled=True)


def gather_directly(x, axis, dim):
    return joined_along(sent_to_all(x, axis), dim)


def split_up(x, dim, size):
    shape = x.shape
    parts = x.reshape(*shape[:dim], size, shape[dim] // size, *shape[dim + 1 :])
    return jnp.moveaxis(parts, dim, 0)


def summed_on_arrival(x, axis, dim):
    size = lax.axis_size(axis)
    parts = lax.all_to_all(split_up(x, dim, size), axis, 0, 0, tiled=True)
    return jnp.sum(parts, axis=0)


def masked_tile(weight_tile, mask_tile):
    rows = weight_tile.shape[0]
    cols = weight_tile.shape[1]
    shaped = weight_tile.reshape(rows // BLOCK, BLOCK, cols // BLOCK, BLOCK)
    factor = mask_tile.astype(jnp.bfloat16)[:, None, :, None]
    return (shaped * factor).reshape(rows, cols)


def per_device(grad_output, inputs, weight, block_mask):
    grads_all = lax.all_gather(grad_output, "col", axis=0, tiled=True)
    inputs_all = gather_directly(inputs, "row", 0)
    tile_cols = weight.shape[1] // BLOCK
    mask_tile = lax.dynamic_slice_in_dim(
        block_mask, lax.axis_index("row") * tile_cols, tile_cols, 1
    )
    kept_tile = masked_tile(weight, mask_tile)
    partial_value = lax.dot_general(
        grads_all, kept_tile, (((1,), (1,)), ((), ())), preferred_element_type=jnp.float32
    )
    grad_input = summed_on_arrival(partial_value, "row", 0).astype(jnp.bfloat16)
    product = lax.dot_general(
        inputs_all, grads_all, (((0,), (0,)), ((), ())), preferred_element_type=jnp.float32
    )
    rows = product.shape[0]
    cols = product.shape[1]
    factor = mask_tile.astype(jnp.float32)[:, None, :, None]
    grad_weight = (
        (product.reshape(rows // BLOCK, BLOCK, cols // BLOCK, BLOCK) * factor)
        .reshape(rows, cols)
        .astype(jnp.bfloat16)
    )
    return (grad_input, grad_weight)


def solution(mesh):
    return jax.shard_map(
        per_device,
        mesh=mesh,
        in_specs=(P("col", "row"), P("row", "col"), P("col", "row"), P("col", None)),
        out_specs=(P("row", "col"), P("col", "row")),
        check_vma=False,
    )
```

profile of v0, /device:TPU:1, one launch (start us, length us, event | category | flops | bytes accessed | tf_op | source)
XLA Modules:
  0.0 135.1 jit_solution(849341611892757135)
XLA Ops:
  7.2 0.0 all-gather.2.cloned.1.call-start
  7.2 0.7 all-gather.2.cloned.1.call-update
  7.9 1.1 copy.19
  9.0 1.5 %broadcast_in_dim.2 = bf16[8,128,896]{1,2,0:T(8,128)(2,1)} broadcast(bf16[128,896]{0,1:T(8,128)(2,1)S(1)} %copy.19), dimensions={1,2} | broadcast | bytes 2064384 | tf_op jit(solution)/shard_map/broadcast_in_dim | solution.py:17
  10.5 6.5 %all-to-all-start.1 = ((bf16[8,128,896]{1,2,0:T(8,128)(2,1)}), bf16[8,128,896]{1,2,0:T(8,128)(2,1)S(1)}, u32[]{:S(2)}, u32[]{:S(2)}) async-start(bf16[8,128,896]{1,2,0:T(8,128)(2,1)} %broadcast_in_dim.2), calls=%async_computation.1 | async-start | bytes 3670016 | tf_op jit(solution)/shard_map/all_to_all | solution.py:17
  17.0 0.0 copy-done.1
  17.0 0.1 dynamic-slice_convert_fusion
  17.1 52.6 %all-gather.2.cloned.1.call-done = bf16[1024,1024]{1,0:T(8,128)(2,1)} async-done(((bf16[32,1024]{1,0:T(8,128)(2,1)}), bf16[1024,1024]{1,0:T(8,128)(2,1)}) %all-gather.2.cloned.1.call-update) | async-done | bytes 2097168 | tf_op jit(solution)/shard_map/all_gather | solution.py:45
  69.7 0.3 mul.23
  70.0 1.2 copy-done.2
  71.2 3.7 %convolution_bitcast_fusion = f32[112,8,8,128]{3,2,1,0:T(8,128)S(1)} fusion(bf16[1024,1024]{1,0:T(8,128)(2,1)} %all-gather.2.cloned.1.call-done, bf16[896,1024]{1,0:T(8,128)(2,1)S(1)} %copy-done.2, bf16[112,8,8,128]{3,2,1,0:T(8,128)(2,1)S(1)} %bitcast.38), kind=kOutput, calls=%fused_computation.2 | convolution fusion | flops 1879965696 | bytes 9437184 | tf_op jit(solution)/shard_map/dot_general | solution.py:52
  74.9 2.1 %copy.36 = f32[112,8,8,128]{3,2,0,1:T(8,128)} copy(f32[112,8,8,128]{3,2,1,0:T(8,128)S(1)} %convolution_bitcast_fusion) | data formatting | bytes 7340032 | tf_op jit(solution)/shard_map/reshape | solution.py:26
  77.0 0.0 all-to-all-done.1
  77.0 4.5 %all-to-all-start = ((f32[8,128,896]{1,2,0:T(8,128)}), f32[8,128,896]{1,2,0:T(8,128)}, u32[]{:S(2)}, u32[]{:S(2)}) async-start(f32[8,128,896]{1,2,0:T(8,128)} %bitcast.31), calls=%async_computation | async-start | bytes 7340032 | tf_op jit(solution)/shard_map/all_to_all | solution.py:32
  81.5 2.6 %copy.20 = bf16[8,128,896]{2,1,0:T(8,128)(2,1)} copy(bf16[8,128,896]{1,2,0:T(8,128)(2,1)S(1)} %all-to-all-done.1) | data formatting | bytes 3670016 | tf_op jit(solution)/shard_map/all_to_all | solution.py:17
  84.1 4.0 %copy.21 = bf16[896,1024]{1,0:T(8,128)(2,1)} copy(bf16[896,1024]{0,1:T(8,128)(2,1)} %bitcast.32) | data formatting | bytes 3670016 | tf_op jit(solution)/shard_map/dot_general | solution.py:56
  88.1 0.0 copy-done
  88.1 2.6 %copy.22 = bf16[1024,1024]{1,0:T(8,128)(2,1)} copy(bf16[1024,1024]{0,1:T(8,128)(2,1)S(1)} %bitcast.34) | data formatting | bytes 4194304 | tf_op jit(solution)/shard_map/dot_general | solution.py:56
  90.7 4.2 %multiply_convert_fusion = bf16[7,128,8,128]{3,1,2,0:T(8,128)(2,1)S(1)} fusion(bf16[7,128,1024,1]{2,1,3,0:T(8,128)(2,1)} %bitcast.37, bf16[8,128,1024,1]{2,1,0,3:T(8,128)(2,1)} %bitcast.35, f32[7,8]{1,0:T(8,128)S(1)} %get-tuple-element.6), kind=kOutput, calls=%fused_computation.1 | convolution fusion | flops 1880883200 | bytes 5767392 | tf_op jit(solution)/shard_map/dot_general | solution.py:56
  95.0 1.2 copy.23
  96.2 1.8 %copy.37 = bf16[112,8,8,128]{3,1,2,0:T(8,128)(2,1)} copy(bf16[112,8,8,128]{3,2,1,0:T(8,128)(2,1)S(1)} %bitcast.33) | data formatting | bytes 3670016
  97.9 27.2 %all-to-all-done = f32[8,128,896]{1,2,0:T(8,128)} async-done(((f32[8,128,896]{1,2,0:T(8,128)}), f32[8,128,896]{1,2,0:T(8,128)}, u32[]{:S(2)}, u32[]{:S(2)}) %all-to-all-start) | async-done | bytes 3670048 | tf_op jit(solution)/shard_map/all_to_all | solution.py:32
  125.2 2.2 %reduce_sum.9 = bf16[128,896]{0,1:T(8,128)(2,1)S(1)} reduce(f32[8,128,896]{1,2,0:T(8,128)} %all-to-all-done, f32[]{:T(128)} %constant.13.clone.1), dimensions={0}, to_apply=%region_0.0 | reduce | flops 802816 | bytes 3899396 | tf_op jit(solution)/shard_map/reduce_sum | solution.py:33
  127.4 0.8 copy.24
  (3 shorter events, 0.0 us)
Async XLA Ops:
  7.2 62.5 %all-gather.2.cloned.1.call-start = ((), (), s32[]{:S(2)}) async-start(), calls=%async_computation.2 | async-start | bytes 2162688 | tf_op jit(solution)/shard_map/all_gather | solution.py:45
  10.5 6.5 %copy-start.1 = (s32[7,64]{1,0:T(8,128)S(1)}, s32[7,64]{1,0:T(8,128)}, u32[]{:S(2)}) copy-start(s32[7,64]{1,0:T(8,128)} %param.7) | copy-start | bytes 5380
  10.5 66.5 %all-to-all-start.1 = ((bf16[8,128,896]{1,2,0:T(8,128)(2,1)}), bf16[8,128,896]{1,2,0:T(8,128)(2,1)S(1)}, u32[]{:S(2)}, u32[]{:S(2)}) async-start(bf16[8,128,896]{1,2,0:T(8,128)(2,1)} %broadcast_in_dim.2), calls=%async_computation.1 | async-start | bytes 3670016 | tf_op jit(solution)/shard_map/all_to_all | solution.py:17
  69.7 1.5 %copy-start.2 = (bf16[896,1024]{1,0:T(8,128)(2,1)S(1)}, bf16[896,1024]{1,0:T(8,128)(2,1)}, u32[]{:S(2)}) copy-start(bf16[896,1024]{1,0:T(8,128)(2,1)} %param.6) | copy-start | bytes 5505028
  77.0 48.2 %all-to-all-start = ((f32[8,128,896]{1,2,0:T(8,128)}), f32[8,128,896]{1,2,0:T(8,128)}, u32[]{:S(2)}, u32[]{:S(2)}) async-start(f32[8,128,896]{1,2,0:T(8,128)} %bitcast.31), calls=%async_computation | async-start | bytes 7340032 | tf_op jit(solution)/shard_map/all_to_all | solution.py:32
  84.1 4.0 %copy-start = (bf16[1024,1024]{1,0:T(8,128)(2,1)S(1)}, bf16[1024,1024]{1,0:T(8,128)(2,1)}, u32[]{:S(2)}) copy-start(bf16[1024,1024]{1,0:T(8,128)(2,1)} %all-gather.2.cloned.1.call-done) | copy-start | bytes 6291460
Sparse Core Ops, SparseCore 0:
  10.5 59.1 all-gather.1
where the time goes:
time: 135 us
  waiting for transfers between devices  80.5 us (60%)
  local copies, waits for them, and re-layouts  19.1 us (14%)
  between operations  14.1 us (10%)
  starting transfers between devices  11 us (8%)
  matrix products  7.99 us (6%)
  other arithmetic  2.3 us (2%)
    all_gather x1, waiting for transfers between devices, per_device(): grads_all = lax.all_gather(grad_output, 'col', axis=0, tiled=True)  52.6 us
    all_to_all x1, waiting for transfers between devices, summed_on_arrival(): parts = lax.all_to_all(split_up(x, dim, size), axis, 0, 0, tiled=True)  27.2 us
    dot_general x2, local copies, waits for them, and re-layouts, per_device(): lax.dot_general(inputs_all, grads_all, (((0,), (0,)), ((), ())), preferre...  6.57 us
    all_to_all x1, starting transfers between devices, sent_to_all(): lax.all_to_all(jnp.broadcast_to(x[None], (size, *x.shape)), axis, 0, 0, t...  6.49 us
    unnamed x9, local copies, waits for them, and re-layouts  4.9 us
    all_to_all x1, starting transfers between devices, summed_on_arrival(): parts = lax.all_to_all(split_up(x, dim, size), axis, 0, 0, tiled=True)  4.5 us
    dot_general x1, matrix products, per_device(): lax.dot_general(inputs_all, grads_all, (((0,), (0,)), ((), ())), preferre...  4.25 us
    dot_general x1, matrix products, per_device(): lax.dot_general(grads_all, kept_tile, (((1,), (1,)), ((), ())), preferred...  3.75 us
  transfers between devices with their start and end apart: 3, of which 2 were waited for; matrix products, arithmetic and copies ran while one was open for 19% of the time, Pallas kernels for 0%

commit v1 on v0

--- a/solution.py
+++ b/solution.py
@@ -42,7 +42,9 @@
 
 
 def per_device(grad_output, inputs, weight, block_mask):
-    grads_all = lax.all_gather(grad_output, "col", axis=0, tiled=True)
+    grads_all = jnp.concatenate(
+        lax.all_to_all(jnp.stack([grad_output] * lax.axis_size("col")), "col", 0, 0), axis=0
+    )
     inputs_all = gather_directly(inputs, "row", 0)
     tile_cols = weight.shape[1] // BLOCK
     mask_tile = lax.dynamic_slice_in_dim(

time: 135 us -> 149 us (1.10)
  between operations: 14.1 us -> 0.71 us
  starting transfers between devices: 11 us -> 24.2 us
  waiting for transfers between devices: 80.5 us -> 92.5 us
  local copies, waits for them, and re-layouts: 19.1 us -> 21.6 us
  matrix products: 7.99 us -> 6.39 us
    all_gather x1 -> x0, waiting for transfers between devices: 52.6 us -> none  [per_device(): grads_all = lax.all_gather(grad_output, 'col', axis=0, tiled=True)]
    all_to_all x0 -> x1, waiting for transfers between devices: none -> 49.4 us  [per_device(): lax.all_to_all(jnp.stack([grad_output] * lax.axis_size('col')), 'col', 0, 0)]
    all_to_all x1, waiting for transfers between devices: 0.01 us -> 18 us  [sent_to_all(): lax.all_to_all(jnp.broadcast_to(x[None], (size, *x.shape)), axis, 0, 0, t...]
    all_to_all x0 -> x1, starting transfers between devices: none -> 12.7 us  [per_device(): lax.all_to_all(jnp.stack([grad_output] * lax.axis_size('col')), 'col', 0, 0)]
    another operation x0 -> x1, local copies, waits for them, and re-layouts: none -> 2.45 us  [per_device(): jnp.stack([grad_output] * lax.axis_size('col'))]
    all_to_all x1, waiting for transfers between devices: 27.2 us -> 25.1 us  [summed_on_arrival(): parts = lax.all_to_all(split_up(x, dim, size), axis, 0, 0, tiled=True)]
    dot_general x1, matrix products: 3.75 us -> 2.15 us  [per_device(): lax.dot_general(grads_all, kept_tile, (((1,), (1,)), ((), ())), preferred...]
  transfers between devices with their start and end apart: 3 -> 3, of which waited for: 2 -> 3; matrix products, arithmetic and copies ran while one was open for 19% -> 15% of each run, Pallas kernels for 0% -> 0%
where the time goes in v1:
time: 149 us; the launch traced here: 148 us
  waiting for transfers between devices  92.5 us (62%)
  starting transfers between devices  24.2 us (16%)
  local copies, waits for them, and re-layouts  21.6 us (14%)
  matrix products  6.39 us (4%)
  other arithmetic  2.3 us (2%)
    all_to_all x1, waiting for transfers between devices, per_device(): lax.all_to_all(jnp.stack([grad_output] * lax.axis_size('col')), 'col', 0, 0)  49.4 us
    all_to_all x1, waiting for transfers between devices, summed_on_arrival(): parts = lax.all_to_all(split_up(x, dim, size), axis, 0, 0, tiled=True)  25.1 us
    all_to_all x1, waiting for transfers between devices, sent_to_all(): lax.all_to_all(jnp.broadcast_to(x[None], (size, *x.shape)), axis, 0, 0, t...  18 us
    all_to_all x1, starting transfers between devices, per_device(): lax.all_to_all(jnp.stack([grad_output] * lax.axis_size('col')), 'col', 0, 0)  12.7 us
    all_to_all x1, starting transfers between devices, sent_to_all(): lax.all_to_all(jnp.broadcast_to(x[None], (size, *x.shape)), axis, 0, 0, t...  7.02 us
    dot_general x2, local copies, waits for them, and re-layouts, per_device(): lax.dot_general(inputs_all, grads_all, (((0,), (0,)), ((), ())), preferre...  6.4 us
    all_to_all x1, starting transfers between devices, summed_on_arrival(): parts = lax.all_to_all(split_up(x, dim, size), axis, 0, 0, tiled=True)  4.49 us
    dot_general x1, matrix products, per_device(): lax.dot_general(inputs_all, grads_all, (((0,), (0,)), ((), ())), preferre...  4.25 us
  transfers between devices with their start and end apart: 3, of which 3 were waited for; matrix products, arithmetic and copies ran while one was open for 15% of the time, Pallas kernels for 0%

profile of v1, /device:TPU:1, one launch (start us, length us, event | category | flops | bytes accessed | tf_op | source)
XLA Modules:
  0.0 147.7 jit_solution(18443043076820855471)
XLA Ops:
  0.6 2.5 %stack.2 = bf16[32,32,1024]{2,1,0:T(8,128)(2,1)} broadcast(bf16[32,1024]{1,0:T(8,128)(2,1)} %param.4), dimensions={1,2} | broadcast | bytes 2162688 | tf_op jit(solution)/shard_map/stack | solution.py:46
  3.1 12.7 %all-to-all-start = ((bf16[32,32,1024]{2,1,0:T(8,128)(2,1)}), bf16[32,32,1024]{2,1,0:T(8,128)(2,1)S(1)}, u32[]{:S(2)}, u32[]{:S(2)}) async-start(bf16[32,32,1024]{2,1,0:T(8,128)(2,1)} %stack.2), calls=%async_computation | async-start | bytes 4194304 | tf_op jit(solution)/shard_map/all_to_all | solution.py:46
  15.8 0.2 copy.19
  16.0 49.4 %all-to-all-done = bf16[32,32,1024]{2,1,0:T(8,128)(2,1)S(1)} async-done(((bf16[32,32,1024]{2,1,0:T(8,128)(2,1)}), bf16[32,32,1024]{2,1,0:T(8,128)(2,1)S(1)}, u32[]{:S(2)}, u32[]{:S(2)}) %all-to-all-start) | async-done | bytes 2097184 | tf_op jit(solution)/shard_map/all_to_all | solution.py:46
  65.4 1.5 broadcast_in_dim.2
  66.9 7.0 %all-to-all-start.2 = ((bf16[8,128,896]{1,2,0:T(8,128)(2,1)}), bf16[8,128,896]{1,2,0:T(8,128)(2,1)}, u32[]{:S(2)}, u32[]{:S(2)}) async-start(bf16[8,128,896]{1,2,0:T(8,128)(2,1)} %broadcast_in_dim.2), calls=%async_computation.2 | async-start | bytes 3670016 | tf_op jit(solution)/shard_map/all_to_all | solution.py:17
  73.9 0.0 copy-done.1
  73.9 0.0 copy-start.2
  73.9 0.1 dynamic-slice_convert_fusion
  74.0 0.3 mul.23
  74.3 1.1 copy-done.2
  75.4 2.1 %convolution_bitcast_fusion = f32[112,8,8,128]{3,2,1,0:T(8,128)S(1)} fusion(bf16[1024,1024]{1,0:T(8,128)(2,1)S(1)} %bitcast.34, bf16[896,1024]{1,0:T(8,128)(2,1)S(1)} %copy-done.2, bf16[112,8,8,128]{3,2,1,0:T(8,128)(2,1)S(1)} %bitcast.41), kind=kOutput, calls=%fused_computation.2 | convolution fusion | flops 1879965696 | bytes 9437184 | tf_op jit(solution)/shard_map/dot_general | solution.py:54
  77.6 2.1 %copy.36 = f32[112,8,8,128]{3,2,0,1:T(8,128)} copy(f32[112,8,8,128]{3,2,1,0:T(8,128)S(1)} %convolution_bitcast_fusion) | data formatting | bytes 7340032 | tf_op jit(solution)/shard_map/reshape | solution.py:26
  79.6 18.0 %all-to-all-done.2 = bf16[8,128,896]{1,2,0:T(8,128)(2,1)} async-done(((bf16[8,128,896]{1,2,0:T(8,128)(2,1)}), bf16[8,128,896]{1,2,0:T(8,128)(2,1)}, u32[]{:S(2)}, u32[]{:S(2)}) %all-to-all-start.2) | async-done | bytes 1835040 | tf_op jit(solution)/shard_map/all_to_all | solution.py:17
  97.6 4.5 %all-to-all-start.1 = ((f32[8,128,896]{1,2,0:T(8,128)}), f32[8,128,896]{1,2,0:T(8,128)}, u32[]{:S(2)}, u32[]{:S(2)}) async-start(f32[8,128,896]{1,2,0:T(8,128)} %bitcast.33), calls=%async_computation.1 | async-start | bytes 7340032 | tf_op jit(solution)/shard_map/all_to_all | solution.py:32
  102.1 3.8 %copy.20 = bf16[8,128,896]{2,1,0:T(8,128)(2,1)} copy(bf16[8,128,896]{1,2,0:T(8,128)(2,1)} %all-to-all-done.2) | data formatting | bytes 3670016 | tf_op jit(solution)/shard_map/all_to_all | solution.py:17
  105.9 3.8 %copy.21 = bf16[896,1024]{1,0:T(8,128)(2,1)} copy(bf16[896,1024]{0,1:T(8,128)(2,1)} %bitcast.36) | data formatting | bytes 3670016 | tf_op jit(solution)/shard_map/dot_general | solution.py:58
  109.7 2.6 %copy.22 = bf16[1024,1024]{1,0:T(8,128)(2,1)} copy(bf16[1024,1024]{0,1:T(8,128)(2,1)S(1)} %bitcast.35) | data formatting | bytes 4194304 | tf_op jit(solution)/shard_map/dot_general | solution.py:58
  112.3 4.2 %multiply_convert_fusion = bf16[7,128,8,128]{3,1,2,0:T(8,128)(2,1)S(1)} fusion(bf16[7,128,1024,1]{2,1,3,0:T(8,128)(2,1)} %bitcast.40, bf16[8,128,1024,1]{2,1,0,3:T(8,128)(2,1)} %bitcast.38, f32[7,8]{1,0:T(8,128)S(1)} %get-tuple-element.6), kind=kOutput, calls=%fused_computation.1 | convolution fusion | flops 1880883200 | bytes 5767392 | tf_op jit(solution)/shard_map/dot_general | solution.py:58
  116.6 1.2 copy.23
  117.8 1.8 %copy.37 = bf16[112,8,8,128]{3,1,2,0:T(8,128)(2,1)} copy(bf16[112,8,8,128]{3,2,1,0:T(8,128)(2,1)S(1)} %bitcast.37) | data formatting | bytes 3670016
  119.5 25.1 %all-to-all-done.1 = f32[8,128,896]{1,2,0:T(8,128)} async-done(((f32[8,128,896]{1,2,0:T(8,128)}), f32[8,128,896]{1,2,0:T(8,128)}, u32[]{:S(2)}, u32[]{:S(2)}) %all-to-all-start.1) | async-done | bytes 3670048 | tf_op jit(solution)/shard_map/all_to_all | solution.py:32
  144.6 2.2 %reduce_sum.9 = bf16[128,896]{0,1:T(8,128)(2,1)S(1)} reduce(f32[8,128,896]{1,2,0:T(8,128)} %all-to-all-done.1, f32[]{:T(128)} %constant.13.clone.1), dimensions={0}, to_apply=%region_0.0 | reduce | flops 802816 | bytes 3899396 | tf_op jit(solution)/shard_map/reduce_sum | solution.py:33
  146.8 0.8 copy.24
  (3 shorter events, 0.0 us)
Async XLA Ops:
  3.1 12.7 %copy-start = (bf16[128,896]{1,0:T(8,128)(2,1)S(1)}, bf16[128,896]{1,0:T(8,128)(2,1)}, u32[]{:S(2)}) copy-start(bf16[128,896]{1,0:T(8,128)(2,1)} %param.5) | copy-start | bytes 688132
  3.1 62.3 %all-to-all-start = ((bf16[32,32,1024]{2,1,0:T(8,128)(2,1)}), bf16[32,32,1024]{2,1,0:T(8,128)(2,1)S(1)}, u32[]{:S(2)}, u32[]{:S(2)}) async-start(bf16[32,32,1024]{2,1,0:T(8,128)(2,1)} %stack.2), calls=%async_computation | async-start | bytes 4194304 | tf_op jit(solution)/shard_map/all_to_all | solution.py:46
  66.9 7.0 %copy-start.1 = (s32[7,64]{1,0:T(8,128)S(1)}, s32[7,64]{1,0:T(8,128)}, u32[]{:S(2)}) copy-start(s32[7,64]{1,0:T(8,128)} %param.7) | copy-start | bytes 5380
  66.9 30.8 %all-to-all-start.2 = ((bf16[8,128,896]{1,2,0:T(8,128)(2,1)}), bf16[8,128,896]{1,2,0:T(8,128)(2,1)}, u32[]{:S(2)}, u32[]{:S(2)}) async-start(bf16[8,128,896]{1,2,0:T(8,128)(2,1)} %broadcast_in_dim.2), calls=%async_computation.2 | async-start | bytes 3670016 | tf_op jit(solution)/shard_map/all_to_all | solution.py:17
  73.9 1.5 %copy-start.2 = (bf16[896,1024]{1,0:T(8,128)(2,1)S(1)}, bf16[896,1024]{1,0:T(8,128)(2,1)}, u32[]{:S(2)}) copy-start(bf16[896,1024]{1,0:T(8,128)(2,1)} %param.6) | copy-start | bytes 5505028
  97.6 47.0 %all-to-all-start.1 = ((f32[8,128,896]{1,2,0:T(8,128)}), f32[8,128,896]{1,2,0:T(8,128)}, u32[]{:S(2)}, u32[]{:S(2)}) async-start(f32[8,128,896]{1,2,0:T(8,128)} %bitcast.33), calls=%async_computation.1 | async-start | bytes 7340032 | tf_op jit(solution)/shard_map/all_to_all | solution.py:32
